TPU v7x, 32 devices: a whole 2x2x4 slice. The times are simulated.
32 devices in a mesh: gz: 8 (over z, y), xy: 4 (over x, core).
Axes of the slice: x: 2, y: 2, z: 4, core: 2. Of those that a mesh axis runs over, the one named last changes fastest.
Arguments:
- volume: float32 [128, 128, 128], P('gz', 'xy'), may hold values from -6 to 6
- owners: int32 [4, 32, 1], P('xy', 'gz'), may hold values from 0 to 7; in each aligned block of 4 rows (0 to 3, 4 to 7, ..., all dimensions but the last counted through in order) at most 2 rows name the same one
Outputs:
- denoised: float32 [128, 128, 128], P('gz', 'xy')
- routed: float32 [4, 128, 128, 128], P('xy', 'gz')
Inputs may be any that keep to these rules, and one draw needn't show every extreme that they name: `owners`: among the 4 blocks of one device no destination is named more than 2 times, a bound that some block reaches.
All inputs are finite; a program needn't handle non-finite values.
Results may differ from a plain program's by a relative error of at most 0.0003.
Values sent between devices are 32-bit elements; how exact they have to be, the bound alone decides.
No kernel may reach another device: no remote copies, remote signals or barrier semaphores. Data moves between devices by JAX's collectives and lax.ppermute only.
A program may use at most 64 MiB of HBM per device.

v0:
```python
import jax
import jax.numpy as jnp
from jax import lax
from jax.sharding import PartitionSpec as P

STEPS = 2
MOST = 2
BLOCK_ROWS = 128
TIME_STEP = 30.0
CONTRAST = 4.0


def with_halo(block, sides, width):
    for axis, dim in sides:
        count = lax.axis_size(axis)
        forward = [(i, i + 1) for i in range(count - 1)]
        backward = [(target, source) for source, target in forward]
        low = lax.ppermute(
            lax.slice_in_dim(block, block.shape[dim] - width, None, axis=dim), axis, forward
        )
        high = lax.ppermute(lax.slice_in_dim(block, 0, width, axis=dim), axis, backward)
        block = jnp.concatenate([low, block, high], axis=dim)
    return block


def shifted(field, stride, line_axis, fill, before):
    length = field.shape[line_axis]
    shape = list(field.shape)
    shape[line_axis] = stride
    padding = jnp.full(tuple(shape), fill, field.dtype)
    if before:
        return jnp.concatenate(
            [padding, lax.slice_in_dim(field, 0, length - stride, axis=line_axis)], axis=line_axis
        )
    return jnp.concatenate(
        [lax.slice_in_dim(field, stride, length, axis=line_axis), padding], axis=line_axis
    )


def cyclic_solve(low_diag, main_diag, high_diag, right_side, line_axis, side_axis):
    length = main_diag.shape[line_axis]
    stride = 1
    while stride < length:
        low_prev = shifted(low_diag, stride, line_axis, 0.0, True)
        main_prev = shifted(main_diag, stride, line_axis, 1.0, True)
        high_prev = shifted(high_diag, stride, line_axis, 0.0, True)
        side_prev = shifted(right_side, stride, side_axis, 0.0, True)
        low_next = shifted(low_diag, stride, line_axis, 0.0, False)
        main_next = shifted(main_diag, stride, line_axis, 1.0, False)
        high_next = shifted(high_diag, stride, line_axis, 0.0, False)
        side_next = shifted(right_side, stride, side_axis, 0.0, False)
        factor_low = -low_diag / main_prev
        factor_high = -high_diag / main_next
        main_diag = main_diag + factor_low * high_prev + factor_high * low_next
        right_side = right_side + factor_low * side_prev + factor_high * side_next
        low_diag = factor_low * low_prev
        high_diag = factor_high * high_next
        stride = stride * 2
    return right_side / main_diag


def coefficients(g_line, line_axis, has_before, has_after):
    length = g_line.shape[line_axis] - 2
    weight = 0.5 * (
        lax.slice_in_dim(g_line, 0, length + 1, axis=line_axis)
        + lax.slice_in_dim(g_line, 1, length + 2, axis=line_axis)
    )
    shape = [1] * weight.ndim
    shape[line_axis] = length + 1
    edge_index = lax.broadcasted_iota(jnp.int32, tuple(shape), line_axis)
    keep_mask = jnp.where(edge_index == 0, has_before, 1.0) * jnp.where(
        edge_index == length, has_after, 1.0
    )
    weight = weight * keep_mask
    low_diag = -3.0 * TIME_STEP * lax.slice_in_dim(weight, 0, length, axis=line_axis)
    high_diag = -3.0 * TIME_STEP * lax.slice_in_dim(weight, 1, length + 1, axis=line_axis)
    main_diag = 1.0 - low_diag - high_diag
    return (low_diag, main_diag, high_diag)


def pad_zero(field, line_axis):
    widths = [(0, 0)] * field.ndim
    widths[line_axis] = (1, 1)
    return jnp.pad(field, widths)


def diffusivity(extended, z_start, z_total, y_start, y_total):
    center = extended[1:-1, 1:-1]
    z_index = z_start - 1 + lax.broadcasted_iota(jnp.int32, (center.shape[0], 1, 1), 0)
    z_next = jnp.where(z_index + 1 < z_total, extended[2:, 1:-1], center)
    z_prev = jnp.where(z_index >= 1, extended[:-2, 1:-1], center)
    y_index = y_start - 1 + lax.broadcasted_iota(jnp.int32, (1, center.shape[1], 1), 1)
    y_next = jnp.where(y_index + 1 < y_total, extended[1:-1, 2:], center)
    y_prev = jnp.where(y_index >= 1, extended[1:-1, :-2], center)
    x_next = jnp.concatenate([center[:, :, 1:], center[:, :, -1:]], axis=2)
    x_prev = jnp.concatenate([center[:, :, :1], center[:, :, :-1]], axis=2)
    slope_z = (z_next - z_prev) * 0.5
    slope_y = (y_next - y_prev) * 0.5
    slope_x = (x_next - x_prev) * 0.5
    squares = slope_z * slope_z + slope_y * slope_y + slope_x * slope_x
    return 1.0 / (1.0 + squares / CONTRAST)


def line_solve(g_field, right_side, line_axis):
    low_diag, main_diag, high_diag = coefficients(pad_zero(g_field, line_axis), line_axis, 0.0, 0.0)
    return cyclic_solve(low_diag, main_diag, high_diag, right_side, line_axis, line_axis)


def interface_solve(gathered, position, chain_size):
    parts = tuple((gathered[:, k] for k in range(6)))
    zeros = jnp.zeros_like(parts[0][0])

    def forward(carry, item):
        prev_p, prev_q = carry
        head_y, head_v, head_w, tail_y, tail_v, tail_w = item
        denom = 1.0 - head_v * prev_q
        first_r = (head_y + head_v * prev_p) / denom
        first_s = head_w / denom
        new_p = tail_y + tail_v * (prev_p + prev_q * first_r)
        new_q = tail_v * prev_q * first_s + tail_w
        return ((new_p, new_q), (first_r, first_s, new_p, new_q))

    carry_out, sweep = lax.scan(forward, (zeros, zeros), parts)

    def backward(later_f, item):
        first_r, first_s, new_p, new_q = item
        head_value = first_r + first_s * later_f
        return (head_value, (head_value, new_p + new_q * later_f))

    final_f, (head_values, tail_values) = lax.scan(backward, zeros, sweep, reverse=True)
    left_pick = lax.dynamic_index_in_dim(
        tail_values, jnp.maximum(position - 1, 0), 0, keepdims=False
    )
    right_pick = lax.dynamic_index_in_dim(
        head_values, jnp.minimum(position + 1, chain_size - 1), 0, keepdims=False
    )
    left_value = jnp.where(position > 0, left_pick, 0.0)
    right_value = jnp.where(position < chain_size - 1, right_pick, 0.0)
    return (left_value, right_value)


def split_solve(g_line, right_side, line_axis, position, chain_size, gather_links):
    has_before = (position > 0).astype(jnp.float32)
    has_after = (position < chain_size - 1).astype(jnp.float32)
    low_diag, main_diag, high_diag = coefficients(g_line, line_axis, has_before, has_after)
    length = main_diag.shape[line_axis]
    shape = [1] * 3
    shape[line_axis] = length
    cell_index = lax.broadcasted_iota(jnp.int32, tuple(shape), line_axis)
    first_link = lax.slice_in_dim(low_diag, 0, 1, axis=line_axis)
    last_link = lax.slice_in_dim(high_diag, length - 1, length, axis=line_axis)
    low_local = jnp.where(cell_index == 0, 0.0, low_diag)
    high_local = jnp.where(cell_index == length - 1, 0.0, high_diag)
    left_side = jnp.where(cell_index == 0, -first_link, 0.0)
    right_part = jnp.where(cell_index == length - 1, -last_link, 0.0)
    stacked = jnp.stack([right_side, left_side, right_part])
    solved = cyclic_solve(low_local, main_diag, high_local, stacked, line_axis, line_axis + 1)
    head = lax.index_in_dim(solved, 0, line_axis + 1, keepdims=False)
    tail = lax.index_in_dim(solved, length - 1, line_axis + 1, keepdims=False)
    packed = jnp.concatenate([head, tail], axis=0)
    gathered = gather_links(packed[None])
    left_value, right_value = interface_solve(gathered, position, chain_size)
    return (
        solved[0]
        + solved[1] * jnp.expand_dims(left_value, line_axis)
        + solved[2] * jnp.expand_dims(right_value, line_axis)
    )


def gather_y(packed):
    return lax.all_gather(packed, "xy", axis=0, tiled=True)


def on_device(volume, owners):
    field = volume
    depth, height, width = field.shape
    z_rank = lax.axis_index("gz")
    z_count = lax.axis_size("gz")
    y_rank = lax.axis_index("xy")
    y_count = lax.axis_size("xy")
    for section_index in range(STEPS):
        extended = with_halo(field, (("gz", 0), ("xy", 1)), 2)
        g_ext = diffusivity(
            extended, z_rank * depth, depth * z_count, y_rank * height, height * y_count
        )
        g_own = g_ext[1:-1, 1:-1]
        along_x = line_solve(g_own, field, 2)
        along_y = split_solve(g_ext[1:-1], field, 1, y_rank, y_count, gather_y)
        moved_g, moved_field = (
            lax.all_to_all(g_own, "gz", split_axis=1, concat_axis=0, tiled=True),
            lax.all_to_all(field, "gz", split_axis=1, concat_axis=0, tiled=True),
        )
        along_z = lax.all_to_all(
            line_solve(moved_g, moved_field, 0), "gz", split_axis=0, concat_axis=1, tiled=True
        )
        field = (along_x + along_y + along_z) / 3.0
    blocks = field.reshape(-1, BLOCK_ROWS, width)
    targets = owners.reshape(-1)
    block_count = targets.shape[0]
    same = targets[:, None] == targets[None, :]
    block_iota = jnp.arange(block_count, dtype=jnp.int32)
    earlier = block_iota[:, None] < block_iota[None, :]
    order_rank = jnp.sum((same & earlier).astype(jnp.int32), axis=0)
    slot_index = targets * MOST + order_rank
    outgoing = (
        jnp.zeros((z_count * MOST, BLOCK_ROWS, width), field.dtype).at[slot_index].set(blocks)
    )
    incoming = lax.all_to_all(outgoing, "gz", split_axis=0, concat_axis=0, tiled=True)
    return (field, incoming.reshape(1, z_count * MOST, BLOCK_ROWS, width))


def solution(mesh):
    in_specs = (P("gz", "xy", None), P("xy", "gz", None))
    out_specs = (P("gz", "xy", None), P("xy", "gz", None, None))
    return jax.shard_map(
        on_device, mesh=mesh, in_specs=in_specs, out_specs=out_specs, check_vma=False
    )
```

profile of v0, /device:TPU:0, one launch (start us, length us, event | category | flops | bytes accessed | tf_op | source)
XLA Modules:
  0.0 191.8 jit_solution(1808513915157954361)
XLA Ops:
  0.6 1.8 copy.129
  2.4 7.3 %all-to-all-start = ((f32[16,32,128]{2,0,1:T(8,128)}), f32[16,32,128]{2,0,1:T(8,128)S(1)}, u32[]{:S(2)}, u32[]{:S(2)}) async-start(f32[16,32,128]{2,0,1:T(8,128)} %copy.129), calls=%async_computation | async-start | bytes 524288 | tf_op jit(solution)/shard_map/all_to_all | solution.py:191
  10.8 1.3 collective-permute-start.1
  12.1 4.6 %collective-permute-start = (f32[2,32,128]{2,0,1:T(2,128)S(1)}, f32[2,32,128]{2,0,1:T(2,128)S(1)}, u32[]{:S(2)}, u32[]{:S(2)}) collective-permute-start(f32[2,32,128]{2,0,1:T(2,128)S(1)} %get-tuple-element.1167), channel_id=1, source_target_pairs={{0,4},{4,8},{8,12},{12,16},{16,20},{20,24},{24,28},{1,5},{5,9},{9,... | collective-permute-start | bytes 98312 | tf_op jit(solution)/shard_map/ppermute | solution.py:18
  16.6 1.2 fusion.185
  19.4 1.3 collective-permute-start.2
  20.7 1.3 collective-permute-start.3
  22.0 3.5 %collective-permute-done.3 = f32[20,2,128]{2,0,1:T(8,128)S(1)} collective-permute-done((f32[20,2,128]{2,0,1:T(8,128)S(1)}, f32[20,2,128]{2,0,1:T(8,128)S(1)}, u32[]{:S(2)}, u32[]{:S(2)}) %collective-permute-start.3) | collective-permute-done | bytes 20512 | tf_op jit(solution)/shard_map/ppermute | solution.py:21
  26.9 1.6 fusion.39
  29.7 1.2 fusion.15
  41.8 6.8 %all-gather = f32[24,16,128]{2,1,0:T(8,128)S(1)} all-gather(f32[6,16,128]{2,1,0:T(8,128)S(1)} %pad_maximum_fusion.16), channel_id=2, replica_groups=mesh['gz'=8,'xy'=4] {'xy'}, dimensions={0}, use_global_device_ids=true | all-gather | bytes 245760 | tf_op jit(solution)/shard_map/all_gather | solution.py:171
  49.1 7.3 %all-to-all-start.1 = ((f32[16,32,128]{2,0,1:T(8,128)}), f32[16,32,128]{2,0,1:T(8,128)S(1)}, u32[]{:S(2)}, u32[]{:S(2)}) async-start(f32[16,32,128]{2,0,1:T(8,128)} %slice.1507), calls=%async_computation.1 | async-start | bytes 524288 | tf_op jit(solution)/shard_map/all_to_all | solution.py:190
  56.5 9.1 %all-to-all-done.1 = f32[16,32,128]{2,0,1:T(8,128)S(1)} async-done(((f32[16,32,128]{2,0,1:T(8,128)}), f32[16,32,128]{2,0,1:T(8,128)S(1)}, u32[]{:S(2)}, u32[]{:S(2)}) %all-to-all-start.1) | async-done | bytes 262176 | tf_op jit(solution)/shard_map/all_to_all | solution.py:190
  69.9 3.6 %all-to-all-start.2 = ((f32[128,4,128]{2,1,0:T(4,128)}), f32[128,4,128]{2,1,0:T(4,128)S(1)}, u32[]{:S(2)}, u32[]{:S(2)}) async-start(f32[128,4,128]{2,1,0:T(4,128)} %copy.142), calls=%async_computation.2 | async-start | bytes 524288 | tf_op jit(solution)/shard_map/all_to_all | solution.py:193
  74.5 7.6 %all-to-all-done.2 = f32[128,4,128]{2,1,0:T(4,128)S(1)} async-done(((f32[128,4,128]{2,1,0:T(4,128)}), f32[128,4,128]{2,1,0:T(4,128)S(1)}, u32[]{:S(2)}, u32[]{:S(2)}) %all-to-all-start.2) | async-done | bytes 262176 | tf_op jit(solution)/shard_map/all_to_all | solution.py:193
  85.1 1.3 collective-permute-start.5
  86.4 4.5 %collective-permute-start.4 = (f32[2,32,128]{2,0,1:T(2,128)S(1)}, f32[2,32,128]{2,0,1:T(2,128)S(1)}, u32[]{:S(2)}, u32[]{:S(2)}) collective-permute-start(f32[2,32,128]{2,0,1:T(2,128)S(1)} %get-tuple-element.1035), channel_id=1, source_target_pairs={{0,4},{4,8},{8,12},{12,16},{16,20},{20,24},{24,28},{1,5},{5,9},{9,... | collective-permute-start | bytes 98312 | tf_op jit(solution)/shard_map/ppermute | solution.py:18
  91.0 3.7 %all-to-all-start.3 = ((f32[16,32,128]{2,0,1:T(8,128)}), f32[16,32,128]{2,0,1:T(8,128)S(1)}, u32[]{:S(2)}, u32[]{:S(2)}) async-start(f32[16,32,128]{2,0,1:T(8,128)} %fusion.61), calls=%async_computation.3 | async-start | bytes 524288 | tf_op jit(solution)/shard_map/all_to_all | solution.py:191
  95.4 1.3 collective-permute-start.6
  96.7 1.3 collective-permute-start.7
  98.0 1.2 fusion.119
  99.2 2.7 %collective-permute-done.7 = f32[20,2,128]{2,0,1:T(8,128)S(1)} collective-permute-done((f32[20,2,128]{2,0,1:T(8,128)S(1)}, f32[20,2,128]{2,0,1:T(8,128)S(1)}, u32[]{:S(2)}, u32[]{:S(2)}) %collective-permute-start.7) | collective-permute-done | bytes 20512 | tf_op jit(solution)/shard_map/ppermute | solution.py:21
  103.3 1.6 fusion.26
  107.5 1.2 multiply_add_fusion.3
  110.9 1.2 fusion.17
  112.7 1.3 multiply_add_fusion.35
  120.2 6.8 %all-gather.1 = f32[24,16,128]{2,1,0:T(8,128)S(1)} all-gather(f32[6,16,128]{2,1,0:T(8,128)S(1)} %pad_maximum_fusion.17), channel_id=3, replica_groups=mesh['gz'=8,'xy'=4] {'xy'}, dimensions={0}, use_global_device_ids=true | all-gather | bytes 245760 | tf_op jit(solution)/shard_map/all_gather | solution.py:171
  127.5 6.0 %all-to-all-start.4 = ((f32[16,32,128]{2,0,1:T(8,128)}), f32[16,32,128]{2,0,1:T(8,128)S(1)}, u32[]{:S(2)}, u32[]{:S(2)}) async-start(f32[16,32,128]{2,0,1:T(8,128)} %slice.1684), calls=%async_computation.4 | async-start | bytes 524288 | tf_op jit(solution)/shard_map/all_to_all | solution.py:190
  133.6 9.1 %all-to-all-done.4 = f32[16,32,128]{2,0,1:T(8,128)S(1)} async-done(((f32[16,32,128]{2,0,1:T(8,128)}), f32[16,32,128]{2,0,1:T(8,128)S(1)}, u32[]{:S(2)}, u32[]{:S(2)}) %all-to-all-start.4) | async-done | bytes 262176 | tf_op jit(solution)/shard_map/all_to_all | solution.py:190
  147.0 3.6 %all-to-all-start.5 = ((f32[128,4,128]{2,1,0:T(4,128)}), f32[128,4,128]{2,1,0:T(4,128)S(1)}, u32[]{:S(2)}, u32[]{:S(2)}) async-start(f32[128,4,128]{2,1,0:T(4,128)} %copy.154), calls=%async_computation.5 | async-start | bytes 524288 | tf_op jit(solution)/shard_map/all_to_all | solution.py:193
  151.6 7.5 %all-to-all-done.5 = f32[128,4,128]{2,1,0:T(4,128)S(1)} async-done(((f32[128,4,128]{2,1,0:T(4,128)}), f32[128,4,128]{2,1,0:T(4,128)S(1)}, u32[]{:S(2)}, u32[]{:S(2)}) %all-to-all-start.5) | async-done | bytes 262176 | tf_op jit(solution)/shard_map/all_to_all | solution.py:193
  162.0 28.8 %all_to_all.113 = f32[16,128,128]{2,1,0:T(8,128)S(1)} all-to-all(f32[16,128,128]{2,1,0:T(8,128)S(1)} %scatter_fusion), channel_id=1, replica_groups=mesh['gz'=8,'xy'=4] {'gz'}, dimensions={0} | all-to-all | bytes 2097152 | tf_op jit(solution)/shard_map/all_to_all | solution.py:208
  (351 shorter events, 46.4 us)
Async XLA Ops:
  2.4 46.6 %all-to-all-start = ((f32[16,32,128]{2,0,1:T(8,128)}), f32[16,32,128]{2,0,1:T(8,128)S(1)}, u32[]{:S(2)}, u32[]{:S(2)}) async-start(f32[16,32,128]{2,0,1:T(8,128)} %copy.129), calls=%async_computation | async-start | bytes 524288 | tf_op jit(solution)/shard_map/all_to_all | solution.py:191
  10.8 7.8 %collective-permute-start.1 = (f32[2,32,128]{2,0,1:T(2,128)S(1)}, f32[2,32,128]{2,0,1:T(2,128)S(1)}, u32[]{:S(2)}, u32[]{:S(2)}) collective-permute-start(f32[2,32,128]{2,0,1:T(2,128)S(1)} %get-tuple-element.1168), channel_id=1, source_target_pairs={{4,0},{8,4},{12,8},{16,12},{20,16},{24,20},{28,24},{5,1},{9,5},{13... | collective-permute-start | bytes 98312 | tf_op jit(solution)/shard_map/ppermute | solution.py:21
  12.1 6.6 %collective-permute-start = (f32[2,32,128]{2,0,1:T(2,128)S(1)}, f32[2,32,128]{2,0,1:T(2,128)S(1)}, u32[]{:S(2)}, u32[]{:S(2)}) collective-permute-start(f32[2,32,128]{2,0,1:T(2,128)S(1)} %get-tuple-element.1167), channel_id=1, source_target_pairs={{0,4},{4,8},{8,12},{12,16},{16,20},{20,24},{24,28},{1,5},{5,9},{9,... | collective-permute-start | bytes 98312 | tf_op jit(solution)/shard_map/ppermute | solution.py:18
  17.8 0.7 copy-start.5
  19.4 2.7 %collective-permute-start.2 = (f32[20,2,128]{2,0,1:T(8,128)S(1)}, f32[20,2,128]{2,0,1:T(8,128)S(1)}, u32[]{:S(2)}, u32[]{:S(2)}) collective-permute-start(f32[20,2,128]{2,0,1:T(8,128)S(1)} %get-tuple-element.887), channel_id=1, source_target_pairs={{0,1},{1,2},{2,3},{4,5},{5,6},{6,7},{8,9},{9,10},{10,11},{12,13},{... | collective-permute-start | bytes 61448 | tf_op jit(solution)/shard_map/ppermute | solution.py:18
  20.7 4.8 %collective-permute-start.3 = (f32[20,2,128]{2,0,1:T(8,128)S(1)}, f32[20,2,128]{2,0,1:T(8,128)S(1)}, u32[]{:S(2)}, u32[]{:S(2)}) collective-permute-start(f32[20,2,128]{2,0,1:T(8,128)S(1)} %get-tuple-element.886), channel_id=1, source_target_pairs={{1,0},{2,1},{3,2},{5,4},{6,5},{7,6},{9,8},{10,9},{11,10},{13,12},{... | collective-permute-start | bytes 61448 | tf_op jit(solution)/shard_map/ppermute | solution.py:21
  31.4 1.0 copy-start.1
  49.1 16.6 %all-to-all-start.1 = ((f32[16,32,128]{2,0,1:T(8,128)}), f32[16,32,128]{2,0,1:T(8,128)S(1)}, u32[]{:S(2)}, u32[]{:S(2)}) async-start(f32[16,32,128]{2,0,1:T(8,128)} %slice.1507), calls=%async_computation.1 | async-start | bytes 524288 | tf_op jit(solution)/shard_map/all_to_all | solution.py:190
  69.9 12.2 %all-to-all-start.2 = ((f32[128,4,128]{2,1,0:T(4,128)}), f32[128,4,128]{2,1,0:T(4,128)S(1)}, u32[]{:S(2)}, u32[]{:S(2)}) async-start(f32[128,4,128]{2,1,0:T(4,128)} %copy.142), calls=%async_computation.2 | async-start | bytes 524288 | tf_op jit(solution)/shard_map/all_to_all | solution.py:193
  82.1 1.0 copy-start.2
  85.1 9.6 %collective-permute-start.5 = (f32[2,32,128]{2,0,1:T(2,128)S(1)}, f32[2,32,128]{2,0,1:T(2,128)S(1)}, u32[]{:S(2)}, u32[]{:S(2)}) collective-permute-start(f32[2,32,128]{2,0,1:T(2,128)S(1)} %get-tuple-element.1036), channel_id=1, source_target_pairs={{4,0},{8,4},{12,8},{16,12},{20,16},{24,20},{28,24},{5,1},{9,5},{13... | collective-permute-start | bytes 98312 | tf_op jit(solution)/shard_map/ppermute | solution.py:21
  86.4 8.3 %collective-permute-start.4 = (f32[2,32,128]{2,0,1:T(2,128)S(1)}, f32[2,32,128]{2,0,1:T(2,128)S(1)}, u32[]{:S(2)}, u32[]{:S(2)}) collective-permute-start(f32[2,32,128]{2,0,1:T(2,128)S(1)} %get-tuple-element.1035), channel_id=1, source_target_pairs={{0,4},{4,8},{8,12},{12,16},{16,20},{20,24},{24,28},{1,5},{5,9},{9,... | collective-permute-start | bytes 98312 | tf_op jit(solution)/shard_map/ppermute | solution.py:18
  91.0 36.5 %all-to-all-start.3 = ((f32[16,32,128]{2,0,1:T(8,128)}), f32[16,32,128]{2,0,1:T(8,128)S(1)}, u32[]{:S(2)}, u32[]{:S(2)}) async-start(f32[16,32,128]{2,0,1:T(8,128)} %fusion.61), calls=%async_computation.3 | async-start | bytes 524288 | tf_op jit(solution)/shard_map/all_to_all | solution.py:191
  95.4 3.8 %collective-permute-start.6 = (f32[20,2,128]{2,0,1:T(8,128)S(1)}, f32[20,2,128]{2,0,1:T(8,128)S(1)}, u32[]{:S(2)}, u32[]{:S(2)}) collective-permute-start(f32[20,2,128]{2,0,1:T(8,128)S(1)} %get-tuple-element.885), channel_id=1, source_target_pairs={{0,1},{1,2},{2,3},{4,5},{5,6},{6,7},{8,9},{9,10},{10,11},{12,13},{... | collective-permute-start | bytes 61448 | tf_op jit(solution)/shard_map/ppermute | solution.py:18
  96.7 5.2 %collective-permute-start.7 = (f32[20,2,128]{2,0,1:T(8,128)S(1)}, f32[20,2,128]{2,0,1:T(8,128)S(1)}, u32[]{:S(2)}, u32[]{:S(2)}) collective-permute-start(f32[20,2,128]{2,0,1:T(8,128)S(1)} %get-tuple-element.884), channel_id=1, source_target_pairs={{1,0},{2,1},{3,2},{5,4},{6,5},{7,6},{9,8},{10,9},{11,10},{13,12},{... | collective-permute-start | bytes 61448 | tf_op jit(solution)/shard_map/ppermute | solution.py:21
  127.5 15.2 %all-to-all-start.4 = ((f32[16,32,128]{2,0,1:T(8,128)}), f32[16,32,128]{2,0,1:T(8,128)S(1)}, u32[]{:S(2)}, u32[]{:S(2)}) async-start(f32[16,32,128]{2,0,1:T(8,128)} %slice.1684), calls=%async_computation.4 | async-start | bytes 524288 | tf_op jit(solution)/shard_map/all_to_all | solution.py:190
  147.0 12.2 %all-to-all-start.5 = ((f32[128,4,128]{2,1,0:T(4,128)}), f32[128,4,128]{2,1,0:T(4,128)S(1)}, u32[]{:S(2)}, u32[]{:S(2)}) async-start(f32[128,4,128]{2,1,0:T(4,128)} %copy.154), calls=%async_computation.5 | async-start | bytes 524288 | tf_op jit(solution)/shard_map/all_to_all | solution.py:193
  159.2 1.0 copy-start.3
  159.2 1.0 copy-start.4
  160.6 0.7 copy-start
where the time goes:
time: 193 us; the launch traced here: 192 us
  starting transfers between devices  48.3 us (25%)
  blocking collectives  42.4 us (22%)
  waiting for transfers between devices  39.6 us (21%)
  other arithmetic  30.1 us (16%)
  local copies, waits for them, and re-layouts  28 us (15%)
  between operations  2.95 us (2%)
    all_to_all x1, blocking collectives, on_device(): lax.all_to_all(outgoing, 'gz', split_axis=0, concat_axis=0, tiled=True)  28.8 us
    all_to_all x2, waiting for transfers between devices, on_device(): lax.all_to_all(g_own, 'gz', split_axis=1, concat_axis=0, tiled=True)  18.3 us
    all_to_all x2, waiting for transfers between devices, on_device(): lax.all_to_all(line_solve(moved_g, moved_field, 0), 'gz', split_axis=0, c...  15.1 us
    all_gather x2, blocking collectives, gather_y(): return lax.all_gather(packed, 'xy', axis=0, tiled=True)  13.7 us
    all_to_all x2, starting transfers between devices, on_device(): lax.all_to_all(g_own, 'gz', split_axis=1, concat_axis=0, tiled=True)  13.3 us
    ppermute x4, starting transfers between devices, with_halo(): lax.ppermute(lax.slice_in_dim(block, block.shape[dim] - width, None, axis...  11.7 us
    all_to_all x2, starting transfers between devices, on_device(): lax.all_to_all(field, 'gz', split_axis=1, concat_axis=0, tiled=True)  11 us
    slice x82, local copies, waits for them, and re-layouts, shifted(): lax.slice_in_dim(field, 0, length - stride, axis=line_axis)  9.39 us
  transfers between devices with their start and end apart: 14, of which 6 were waited for; matrix products, arithmetic and copies ran while one was open for 21% of the time, Pallas kernels for 0%

commit v1 on v0

--- a/solution.py
+++ b/solution.py
@@ -168,7 +168,9 @@
 
 
 def gather_y(packed):
-    return lax.all_gather(packed, "xy", axis=0, tiled=True)
+    return jnp.concatenate(
+        lax.all_to_all(jnp.stack([packed] * lax.axis_size("xy")), "xy", 0, 0), axis=0
+    )
 
 
 def on_device(volume, owners):

time: 193 us -> 215 us (1.11)
  waiting for transfers between devices: 39.6 us -> 64.4 us
  blocking collectives: 42.4 us -> 28.7 us
  local copies, waits for them, and re-layouts: 28 us -> 31.6 us
  starting transfers between devices: 48.3 us -> 51.8 us
  other arithmetic: 30.1 us -> 33.1 us
    all_to_all x2, waiting for transfers between devices: 0.01 us -> 15.3 us  [on_device(): lax.all_to_all(field, 'gz', split_axis=1, concat_axis=0, tiled=True)]
    all_gather x2 -> x0, blocking collectives: 13.7 us -> none  [gather_y(): return lax.all_gather(packed, 'xy', axis=0, tiled=True)]
    all_to_all x0 -> x2, waiting for transfers between devices: none -> 8.94 us  [gather_y(): lax.all_to_all(jnp.stack([packed] * lax.axis_size('xy')), 'xy', 0, 0)]
    all_to_all x0 -> x2, starting transfers between devices: none -> 7.65 us  [gather_y(): lax.all_to_all(jnp.stack([packed] * lax.axis_size('xy')), 'xy', 0, 0)]
    all_to_all x2, starting transfers between devices: 13.3 us -> 7.23 us  [on_device(): lax.all_to_all(g_own, 'gz', split_axis=1, concat_axis=0, tiled=True)]
    all_to_all x2, waiting for transfers between devices: 18.3 us -> 16.1 us  [on_device(): lax.all_to_all(g_own, 'gz', split_axis=1, concat_axis=0, tiled=True)]
    unnamed x15 -> x47, local copies, waits for them, and re-layouts: 6.83 us -> 7.62 us
  transfers between devices with their start and end apart: 14 -> 16, of which waited for: 6 -> 11; matrix products, arithmetic and copies ran while one was open for 21% -> 4% of each run, Pallas kernels for 0% -> 0%
where the time goes in v1:
time: 215 us; the launch traced here: 213 us
  waiting for transfers between devices  64.4 us (30%)
  starting transfers between devices  51.8 us (24%)
  other arithmetic  33.1 us (15%)
  local copies, waits for them, and re-layouts  31.6 us (15%)
  blocking collectives  28.7 us (13%)
  between operations  3.09 us (1%)
    all_to_all x1, blocking collectives, on_device(): lax.all_to_all(outgoing, 'gz', split_axis=0, concat_axis=0, tiled=True)  28.7 us
    all_to_all x2, waiting for transfers between devices, on_device(): lax.all_to_all(line_solve(moved_g, moved_field, 0), 'gz', split_axis=0, c...  16.6 us
    all_to_all x2, waiting for transfers between devices, on_device(): lax.all_to_all(g_own, 'gz', split_axis=1, concat_axis=0, tiled=True)  16.1 us
    all_to_all x2, waiting for transfers between devices, on_device(): lax.all_to_all(field, 'gz', split_axis=1, concat_axis=0, tiled=True)  15.3 us
    ppermute x4, starting transfers between devices, with_halo(): lax.ppermute(lax.slice_in_dim(block, block.shape[dim] - width, None, axis...  12.8 us
    all_to_all x2, starting transfers between devices, on_device(): lax.all_to_all(field, 'gz', split_axis=1, concat_axis=0, tiled=True)  11.8 us
    slice x82, local copies, waits for them, and re-layouts, shifted(): lax.slice_in_dim(field, 0, length - stride, axis=line_axis)  10.9 us
    all_to_all x2, waiting for transfers between devices, gather_y(): lax.all_to_all(jnp.stack([packed] * lax.axis_size('xy')), 'xy', 0, 0)  8.94 us
  transfers between devices with their start and end apart: 16, of which 11 were waited for; matrix products, arithmetic and copies ran while one was open for 4% of the time, Pallas kernels for 0%

profile of v1, /device:TPU:0, one launch (start us, length us, event | category | flops | bytes accessed | tf_op | source)
XLA Modules:
  0.0 213.2 jit_solution(2333308066686365730)
XLA Ops:
  0.6 1.8 copy.69
  3.4 1.3 collective-permute-start.1
  4.7 5.5 %collective-permute-start = (f32[2,32,128]{2,0,1:T(2,128)S(1)}, f32[2,32,128]{2,0,1:T(2,128)S(1)}, u32[]{:S(2)}, u32[]{:S(2)}) collective-permute-start(f32[2,32,128]{2,0,1:T(2,128)S(1)} %get-tuple-element.1167), channel_id=1, source_target_pairs={{0,4},{4,8},{8,12},{12,16},{16,20},{20,24},{24,28},{1,5},{5,9},{9,... | collective-permute-start | bytes 98312 | tf_op jit(solution)/shard_map/ppermute | solution.py:18
  13.7 1.5 collective-permute-start.2
  15.1 1.3 collective-permute-start.3
  16.5 3.8 %collective-permute-done.3 = f32[20,2,128]{2,0,1:T(8,128)S(1)} collective-permute-done((f32[20,2,128]{2,0,1:T(8,128)S(1)}, f32[20,2,128]{2,0,1:T(8,128)S(1)}, u32[]{:S(2)}, u32[]{:S(2)}) %collective-permute-start.3) | collective-permute-done | bytes 20512 | tf_op jit(solution)/shard_map/ppermute | solution.py:21
  21.7 1.7 fusion.39
  37.3 3.8 %all-to-all-start = ((f32[4,1,6,16,128]{4,3,2,1,0:T(8,128)}), f32[4,1,6,16,128]{4,3,2,1,0:T(8,128)S(1)}, u32[]{:S(2)}, u32[]{:S(2)}) async-start(f32[4,1,6,16,128]{4,3,2,1,0:T(8,128)} %stack.24), calls=%async_computation | async-start | bytes 393216 | tf_op jit(solution)/shard_map/all_to_all | solution.py:172
  42.0 4.5 %all-to-all-done = f32[4,1,6,16,128]{4,3,2,1,0:T(8,128)S(1)} async-done(((f32[4,1,6,16,128]{4,3,2,1,0:T(8,128)}), f32[4,1,6,16,128]{4,3,2,1,0:T(8,128)S(1)}, u32[]{:S(2)}, u32[]{:S(2)}) %all-to-all-start) | async-done | bytes 196640 | tf_op jit(solution)/shard_map/all_to_all | solution.py:172
  46.5 6.4 %all-to-all-start.1 = ((f32[16,32,128]{2,0,1:T(8,128)}), f32[16,32,128]{2,0,1:T(8,128)S(1)}, u32[]{:S(2)}, u32[]{:S(2)}) async-start(f32[16,32,128]{2,0,1:T(8,128)} %copy.69), calls=%async_computation.1 | async-start | bytes 524288 | tf_op jit(solution)/shard_map/all_to_all | solution.py:193
  53.8 7.6 %all-to-all-done.1 = f32[16,32,128]{2,0,1:T(8,128)S(1)} async-done(((f32[16,32,128]{2,0,1:T(8,128)}), f32[16,32,128]{2,0,1:T(8,128)S(1)}, u32[]{:S(2)}, u32[]{:S(2)}) %all-to-all-start.1) | async-done | bytes 262176 | tf_op jit(solution)/shard_map/all_to_all | solution.py:193
  61.4 3.6 %all-to-all-start.2 = ((f32[16,32,128]{2,0,1:T(8,128)}), f32[16,32,128]{2,0,1:T(8,128)S(1)}, u32[]{:S(2)}, u32[]{:S(2)}) async-start(f32[16,32,128]{2,0,1:T(8,128)} %slice.1507), calls=%async_computation.2 | async-start | bytes 524288 | tf_op jit(solution)/shard_map/all_to_all | solution.py:192
  65.3 8.0 %all-to-all-done.2 = f32[16,32,128]{2,0,1:T(8,128)S(1)} async-done(((f32[16,32,128]{2,0,1:T(8,128)}), f32[16,32,128]{2,0,1:T(8,128)S(1)}, u32[]{:S(2)}, u32[]{:S(2)}) %all-to-all-start.2) | async-done | bytes 262176 | tf_op jit(solution)/shard_map/all_to_all | solution.py:192
  77.6 3.6 %all-to-all-start.3 = ((f32[128,4,128]{2,1,0:T(4,128)}), f32[128,4,128]{2,1,0:T(4,128)S(1)}, u32[]{:S(2)}, u32[]{:S(2)}) async-start(f32[128,4,128]{2,1,0:T(4,128)} %copy.76), calls=%async_computation.3 | async-start | bytes 524288 | tf_op jit(solution)/shard_map/all_to_all | solution.py:195
  81.4 8.3 %all-to-all-done.3 = f32[128,4,128]{2,1,0:T(4,128)S(1)} async-done(((f32[128,4,128]{2,1,0:T(4,128)}), f32[128,4,128]{2,1,0:T(4,128)S(1)}, u32[]{:S(2)}, u32[]{:S(2)}) %all-to-all-start.3) | async-done | bytes 262176 | tf_op jit(solution)/shard_map/all_to_all | solution.py:195
  90.8 2.0 fusion.61
  93.8 1.3 collective-permute-start.5
  95.1 4.5 %collective-permute-start.4 = (f32[2,32,128]{2,0,1:T(2,128)S(1)}, f32[2,32,128]{2,0,1:T(2,128)S(1)}, u32[]{:S(2)}, u32[]{:S(2)}) collective-permute-start(f32[2,32,128]{2,0,1:T(2,128)S(1)} %get-tuple-element.1035), channel_id=1, source_target_pairs={{0,4},{4,8},{8,12},{12,16},{16,20},{20,24},{24,28},{1,5},{5,9},{9,... | collective-permute-start | bytes 98312 | tf_op jit(solution)/shard_map/ppermute | solution.py:18
  103.3 1.3 collective-permute-start.7
  105.8 2.8 %collective-permute-done.7 = f32[20,2,128]{2,0,1:T(8,128)S(1)} collective-permute-done((f32[20,2,128]{2,0,1:T(8,128)S(1)}, f32[20,2,128]{2,0,1:T(8,128)S(1)}, u32[]{:S(2)}, u32[]{:S(2)}) %collective-permute-start.7) | collective-permute-done | bytes 20512 | tf_op jit(solution)/shard_map/ppermute | solution.py:21
  110.7 1.7 fusion.26
  120.1 1.3 multiply_add_fusion.35
  128.3 3.8 %all-to-all-start.4 = ((f32[4,1,6,16,128]{4,3,2,1,0:T(8,128)}), f32[4,1,6,16,128]{4,3,2,1,0:T(8,128)S(1)}, u32[]{:S(2)}, u32[]{:S(2)}) async-start(f32[4,1,6,16,128]{4,3,2,1,0:T(8,128)} %stack.27), calls=%async_computation.4 | async-start | bytes 393216 | tf_op jit(solution)/shard_map/all_to_all | solution.py:172
  133.0 4.5 %all-to-all-done.4 = f32[4,1,6,16,128]{4,3,2,1,0:T(8,128)S(1)} async-done(((f32[4,1,6,16,128]{4,3,2,1,0:T(8,128)}), f32[4,1,6,16,128]{4,3,2,1,0:T(8,128)S(1)}, u32[]{:S(2)}, u32[]{:S(2)}) %all-to-all-start.4) | async-done | bytes 196640 | tf_op jit(solution)/shard_map/all_to_all | solution.py:172
  137.4 5.4 %all-to-all-start.5 = ((f32[16,32,128]{2,0,1:T(8,128)}), f32[16,32,128]{2,0,1:T(8,128)S(1)}, u32[]{:S(2)}, u32[]{:S(2)}) async-start(f32[16,32,128]{2,0,1:T(8,128)} %fusion.61), calls=%async_computation.5 | async-start | bytes 524288 | tf_op jit(solution)/shard_map/all_to_all | solution.py:193
  143.7 7.6 %all-to-all-done.5 = f32[16,32,128]{2,0,1:T(8,128)S(1)} async-done(((f32[16,32,128]{2,0,1:T(8,128)}), f32[16,32,128]{2,0,1:T(8,128)S(1)}, u32[]{:S(2)}, u32[]{:S(2)}) %all-to-all-start.5) | async-done | bytes 262176 | tf_op jit(solution)/shard_map/all_to_all | solution.py:193
  151.3 3.6 %all-to-all-start.6 = ((f32[16,32,128]{2,0,1:T(8,128)}), f32[16,32,128]{2,0,1:T(8,128)S(1)}, u32[]{:S(2)}, u32[]{:S(2)}) async-start(f32[16,32,128]{2,0,1:T(8,128)} %slice.1684), calls=%async_computation.6 | async-start | bytes 524288 | tf_op jit(solution)/shard_map/all_to_all | solution.py:192
  155.3 8.0 %all-to-all-done.6 = f32[16,32,128]{2,0,1:T(8,128)S(1)} async-done(((f32[16,32,128]{2,0,1:T(8,128)}), f32[16,32,128]{2,0,1:T(8,128)S(1)}, u32[]{:S(2)}, u32[]{:S(2)}) %all-to-all-start.6) | async-done | bytes 262176 | tf_op jit(solution)/shard_map/all_to_all | solution.py:192
  167.6 3.6 %all-to-all-start.7 = ((f32[128,4,128]{2,1,0:T(4,128)}), f32[128,4,128]{2,1,0:T(4,128)S(1)}, u32[]{:S(2)}, u32[]{:S(2)}) async-start(f32[128,4,128]{2,1,0:T(4,128)} %copy.82), calls=%async_computation.7 | async-start | bytes 524288 | tf_op jit(solution)/shard_map/all_to_all | solution.py:195
  171.4 8.3 %all-to-all-done.7 = f32[128,4,128]{2,1,0:T(4,128)S(1)} async-done(((f32[128,4,128]{2,1,0:T(4,128)}), f32[128,4,128]{2,1,0:T(4,128)S(1)}, u32[]{:S(2)}, u32[]{:S(2)}) %all-to-all-start.7) | async-done | bytes 262176 | tf_op jit(solution)/shard_map/all_to_all | solution.py:195
  180.7 1.3 fusion.54
  183.5 28.7 %all_to_all.123 = f32[16,128,128]{2,1,0:T(8,128)S(1)} all-to-all(f32[16,128,128]{2,1,0:T(8,128)S(1)} %scatter_fusion), channel_id=1, replica_groups=mesh['gz'=8,'xy'=4] {'gz'}, dimensions={0} | all-to-all | bytes 2097152 | tf_op jit(solution)/shard_map/all_to_all | solution.py:210
  (387 shorter events, 58.0 us)
Async XLA Ops:
  3.4 9.4 %collective-permute-start.1 = (f32[2,32,128]{2,0,1:T(2,128)S(1)}, f32[2,32,128]{2,0,1:T(2,128)S(1)}, u32[]{:S(2)}, u32[]{:S(2)}) collective-permute-start(f32[2,32,128]{2,0,1:T(2,128)S(1)} %get-tuple-element.1168), channel_id=1, source_target_pairs={{4,0},{8,4},{12,8},{16,12},{20,16},{24,20},{28,24},{5,1},{9,5},{13... | collective-permute-start | bytes 98312 | tf_op jit(solution)/shard_map/ppermute | solution.py:21
  4.7 8.2 %collective-permute-start = (f32[2,32,128]{2,0,1:T(2,128)S(1)}, f32[2,32,128]{2,0,1:T(2,128)S(1)}, u32[]{:S(2)}, u32[]{:S(2)}) collective-permute-start(f32[2,32,128]{2,0,1:T(2,128)S(1)} %get-tuple-element.1167), channel_id=1, source_target_pairs={{0,4},{4,8},{8,12},{12,16},{16,20},{20,24},{24,28},{1,5},{5,9},{9,... | collective-permute-start | bytes 98312 | tf_op jit(solution)/shard_map/ppermute | solution.py:18
  10.3 14.1 %copy-start.6 = (pred[32]{0:T(512)(128)(4,1)}, pred[32]{0:T(512)(128)(4,1)S(1)}, u32[]{:S(2)}) copy-start(pred[32]{0:T(512)(128)(4,1)S(1)} %get-tuple-element.1185) | copy-start | bytes 100
  11.5 10.1 %copy-start.8 = (pred[34]{0:T(512)(128)(4,1)}, pred[34]{0:T(512)(128)(4,1)S(1)}, u32[]{:S(2)}) copy-start(pred[34]{0:T(512)(128)(4,1)S(1)} %get-tuple-element.1181) | copy-start | bytes 106
  11.5 10.1 %copy-start.10 = (pred[34]{0:T(512)(128)(4,1)}, pred[34]{0:T(512)(128)(4,1)S(1)}, u32[]{:S(2)}) copy-start(pred[34]{0:T(512)(128)(4,1)S(1)} %get-tuple-element.1182) | copy-start | bytes 106
  12.9 8.8 %copy-start.12 = (pred[18]{0:T(512)(128)(4,1)}, pred[18]{0:T(512)(128)(4,1)S(1)}, u32[]{:S(2)}) copy-start(pred[18]{0:T(512)(128)(4,1)S(1)} %get-tuple-element.1183) | copy-start | bytes 58
  12.9 8.8 %copy-start.14 = (pred[18]{0:T(512)(128)(4,1)}, pred[18]{0:T(512)(128)(4,1)S(1)}, u32[]{:S(2)}) copy-start(pred[18]{0:T(512)(128)(4,1)S(1)} %get-tuple-element.1184) | copy-start | bytes 58
  13.7 2.8 %collective-permute-start.2 = (f32[20,2,128]{2,0,1:T(8,128)S(1)}, f32[20,2,128]{2,0,1:T(8,128)S(1)}, u32[]{:S(2)}, u32[]{:S(2)}) collective-permute-start(f32[20,2,128]{2,0,1:T(8,128)S(1)} %get-tuple-element.887), channel_id=1, source_target_pairs={{0,1},{1,2},{2,3},{4,5},{5,6},{6,7},{8,9},{9,10},{10,11},{12,13},{... | collective-permute-start | bytes 61448 | tf_op jit(solution)/shard_map/ppermute | solution.py:18
  15.1 5.1 %collective-permute-start.3 = (f32[20,2,128]{2,0,1:T(8,128)S(1)}, f32[20,2,128]{2,0,1:T(8,128)S(1)}, u32[]{:S(2)}, u32[]{:S(2)}) collective-permute-start(f32[20,2,128]{2,0,1:T(8,128)S(1)} %get-tuple-element.886), channel_id=1, source_target_pairs={{1,0},{2,1},{3,2},{5,4},{6,5},{7,6},{9,8},{10,9},{11,10},{13,12},{... | collective-permute-start | bytes 61448 | tf_op jit(solution)/shard_map/ppermute | solution.py:21
  16.4 7.6 %copy-start.16 = (f32[33]{0:T(128)}, f32[33]{0:T(128)S(1)}, u32[]{:S(2)}) copy-start(f32[33]{0:T(128)S(1)} %fusion.73) | copy-start | bytes 400
  26.2 1.0 copy-start.1
  37.3 9.1 %all-to-all-start = ((f32[4,1,6,16,128]{4,3,2,1,0:T(8,128)}), f32[4,1,6,16,128]{4,3,2,1,0:T(8,128)S(1)}, u32[]{:S(2)}, u32[]{:S(2)}) async-start(f32[4,1,6,16,128]{4,3,2,1,0:T(8,128)} %stack.24), calls=%async_computation | async-start | bytes 393216 | tf_op jit(solution)/shard_map/all_to_all | solution.py:172
  46.5 14.9 %all-to-all-start.1 = ((f32[16,32,128]{2,0,1:T(8,128)}), f32[16,32,128]{2,0,1:T(8,128)S(1)}, u32[]{:S(2)}, u32[]{:S(2)}) async-start(f32[16,32,128]{2,0,1:T(8,128)} %copy.69), calls=%async_computation.1 | async-start | bytes 524288 | tf_op jit(solution)/shard_map/all_to_all | solution.py:193
  61.4 12.0 %all-to-all-start.2 = ((f32[16,32,128]{2,0,1:T(8,128)}), f32[16,32,128]{2,0,1:T(8,128)S(1)}, u32[]{:S(2)}, u32[]{:S(2)}) async-start(f32[16,32,128]{2,0,1:T(8,128)} %slice.1507), calls=%async_computation.2 | async-start | bytes 524288 | tf_op jit(solution)/shard_map/all_to_all | solution.py:192
  77.6 12.1 %all-to-all-start.3 = ((f32[128,4,128]{2,1,0:T(4,128)}), f32[128,4,128]{2,1,0:T(4,128)S(1)}, u32[]{:S(2)}, u32[]{:S(2)}) async-start(f32[128,4,128]{2,1,0:T(4,128)} %copy.76), calls=%async_computation.3 | async-start | bytes 524288 | tf_op jit(solution)/shard_map/all_to_all | solution.py:195
  89.8 1.0 copy-start.3
  89.8 1.0 copy-start.5
  93.8 5.9 %copy-start.20 = (s32[1,4,1]{1,2,0:T(1,128)S(1)}, s32[1,4,1]{1,2,0:T(1,128)}, u32[]{:S(2)}) copy-start(s32[1,4,1]{1,2,0:T(1,128)} %param.11) | copy-start | bytes 52
  93.8 5.9 %copy-start.21 = (s32[4]{0:T(128)S(1)}, s32[4]{0:T(128)}, u32[]{:S(2)}) copy-start(s32[4]{0:T(128)} %convert_reduce_fusion) | copy-start | bytes 52
  93.8 6.4 %collective-permute-start.5 = (f32[2,32,128]{2,0,1:T(2,128)S(1)}, f32[2,32,128]{2,0,1:T(2,128)S(1)}, u32[]{:S(2)}, u32[]{:S(2)}) collective-permute-start(f32[2,32,128]{2,0,1:T(2,128)S(1)} %get-tuple-element.1036), channel_id=1, source_target_pairs={{4,0},{8,4},{12,8},{16,12},{20,16},{24,20},{28,24},{5,1},{9,5},{13... | collective-permute-start | bytes 98312 | tf_op jit(solution)/shard_map/ppermute | solution.py:21
  95.1 6.1 %collective-permute-start.4 = (f32[2,32,128]{2,0,1:T(2,128)S(1)}, f32[2,32,128]{2,0,1:T(2,128)S(1)}, u32[]{:S(2)}, u32[]{:S(2)}) collective-permute-start(f32[2,32,128]{2,0,1:T(2,128)S(1)} %get-tuple-element.1035), channel_id=1, source_target_pairs={{0,4},{4,8},{8,12},{12,16},{16,20},{20,24},{24,28},{1,5},{5,9},{9,... | collective-permute-start | bytes 98312 | tf_op jit(solution)/shard_map/ppermute | solution.py:18
  102.0 3.8 %collective-permute-start.6 = (f32[20,2,128]{2,0,1:T(8,128)S(1)}, f32[20,2,128]{2,0,1:T(8,128)S(1)}, u32[]{:S(2)}, u32[]{:S(2)}) collective-permute-start(f32[20,2,128]{2,0,1:T(8,128)S(1)} %get-tuple-element.885), channel_id=1, source_target_pairs={{0,1},{1,2},{2,3},{4,5},{5,6},{6,7},{8,9},{9,10},{10,11},{12,13},{... | collective-permute-start | bytes 61448 | tf_op jit(solution)/shard_map/ppermute | solution.py:18
  103.3 5.3 %collective-permute-start.7 = (f32[20,2,128]{2,0,1:T(8,128)S(1)}, f32[20,2,128]{2,0,1:T(8,128)S(1)}, u32[]{:S(2)}, u32[]{:S(2)}) collective-permute-start(f32[20,2,128]{2,0,1:T(8,128)S(1)} %get-tuple-element.884), channel_id=1, source_target_pairs={{1,0},{2,1},{3,2},{5,4},{6,5},{7,6},{9,8},{10,9},{11,10},{13,12},{... | collective-permute-start | bytes 61448 | tf_op jit(solution)/shard_map/ppermute | solution.py:21
  110.7 1.7 copy-start.17
  112.5 0.7 copy-start.7
  128.3 9.1 %all-to-all-start.4 = ((f32[4,1,6,16,128]{4,3,2,1,0:T(8,128)}), f32[4,1,6,16,128]{4,3,2,1,0:T(8,128)S(1)}, u32[]{:S(2)}, u32[]{:S(2)}) async-start(f32[4,1,6,16,128]{4,3,2,1,0:T(8,128)} %stack.27), calls=%async_computation.4 | async-start | bytes 393216 | tf_op jit(solution)/shard_map/all_to_all | solution.py:172
  137.4 13.9 %all-to-all-start.5 = ((f32[16,32,128]{2,0,1:T(8,128)}), f32[16,32,128]{2,0,1:T(8,128)S(1)}, u32[]{:S(2)}, u32[]{:S(2)}) async-start(f32[16,32,128]{2,0,1:T(8,128)} %fusion.61), calls=%async_computation.5 | async-start | bytes 524288 | tf_op jit(solution)/shard_map/all_to_all | solution.py:193
  151.3 12.0 %all-to-all-start.6 = ((f32[16,32,128]{2,0,1:T(8,128)}), f32[16,32,128]{2,0,1:T(8,128)S(1)}, u32[]{:S(2)}, u32[]{:S(2)}) async-start(f32[16,32,128]{2,0,1:T(8,128)} %slice.1684), calls=%async_computation.6 | async-start | bytes 524288 | tf_op jit(solution)/shard_map/all_to_all | solution.py:192
  167.6 12.1 %all-to-all-start.7 = ((f32[128,4,128]{2,1,0:T(4,128)}), f32[128,4,128]{2,1,0:T(4,128)S(1)}, u32[]{:S(2)}, u32[]{:S(2)}) async-start(f32[128,4,128]{2,1,0:T(4,128)} %copy.82), calls=%async_computation.7 | async-start | bytes 524288 | tf_op jit(solution)/shard_map/all_to_all | solution.py:195
  179.7 1.0 copy-start.2
  179.7 1.0 copy-start.4
  182.1 0.7 copy-start
  (6 other events, 3.8 us)
